TPU v7x, 32 devices: a whole 2x2x4 slice. The times are simulated.
32 devices in a mesh: frames: 4 (over x, core), feat: 8 (over z, y).
Axes of the slice: x: 2, y: 2, z: 4, core: 2. Of those that a mesh axis runs over, the one named last changes fastest.
Arguments:
- acoustic: float32 [1024, 440], P('frames'), may hold values from -6 to 6
- projection: float32 [440, 8192], P(None, 'feat'), may hold values from -0.25 to 0.25
- phases: float32 [8192], P('feat'), may hold values from -3.140625 to 3.140625
- labels: int32 [1024], P('frames'), may hold values from 0 to 146
- weights: float32 [147, 8192], P(None, 'feat'), may hold values from -1.5 to 1.5
- scaled_duals: float32 [147, 1024], P(None, 'frames'), may hold values from -7 to 7
Outputs:
- weights_out: float32 [147, 8192], P(None, 'feat')
- duals_out: float32 [147, 1024], P(None, ('frames', 'feat'))
- penalty: float32 [], replicated
All inputs are finite; a program needn't handle non-finite values.
Results may differ from a plain program's by a relative error of at most 0.0003.
Values sent between devices are 32-bit elements; how exact they have to be, the bound alone decides.
No kernel may reach another device: no remote copies, remote signals or barrier semaphores. Data moves between devices by JAX's collectives and lax.ppermute only.
A program may use at most 64 MiB of HBM per device.

v0:
```python
import jax
import jax.numpy as jnp
from jax import lax
from jax.sharding import PartitionSpec as P

ITERS = 2
highest = lax.Precision.HIGHEST
epsilon = 1e-06
ridge_weight = 2.0


def cosine_features(acoustic, projection, phases, total_features):
    mixed = (
        jnp.dot(acoustic, projection, precision=highest, preferred_element_type=jnp.float32)
        + phases[None, :]
    )
    return jnp.sqrt(2.0 / total_features) * jnp.cos(mixed)


def ridge_solve(factor, right):
    middle = lax.linalg.triangular_solve(
        factor, right, left_side=False, lower=True, transpose_a=True
    )
    return lax.linalg.triangular_solve(
        factor, middle, left_side=False, lower=True, transpose_a=False
    )


def proximal(predicted, duals, target, penalty):
    shifted = predicted + duals
    inner = (2.0 * target + penalty * shifted) / (2.0 + penalty)
    split = jnp.where(target * shifted < 1.0, inner, shifted)
    miss = predicted - split
    duals_next = duals + miss
    residual = split - duals_next - predicted
    return (miss, duals_next, residual)


def shards(acoustic, projection, phases, labels, weights, scaled_duals):
    frames_here = acoustic.shape[0]
    block_width = projection.shape[1]
    class_count = weights.shape[0]
    feat_count = lax.axis_size("feat")
    group_count = lax.axis_size("frames")
    total_features = block_width * feat_count
    total_frames = frames_here * group_count
    ridge = frames_here / total_features
    share = frames_here // feat_count
    offset = lax.axis_index("feat") * share
    basis = cosine_features(acoustic, projection, phases, total_features)
    inner_matrix = ridge * jnp.eye(frames_here, dtype=jnp.float32) + lax.dot_general(
        basis, basis, (((1,), (1,)), ((), ())), precision=highest
    )
    factor = jnp.linalg.cholesky(inner_matrix)
    classes = lax.broadcasted_iota(jnp.int32, (class_count, frames_here), 0)
    target = jnp.where(classes == labels[None, :], 1.0, -1.0).astype(jnp.float32)
    duals = scaled_duals
    penalty = jnp.ones((), jnp.float32)
    for iteration in range(ITERS):
        partial_value = lax.dot_general(weights, basis, (((1,), (1,)), ((), ())), precision=highest)
        predicted = lax.psum(partial_value, "feat")
        miss, duals, residual = proximal(predicted, duals, target, penalty)
        mine = lax.dynamic_slice_in_dim(miss, offset, share, 1)
        primal_part = jnp.sum(mine * mine)
        proj = (
            jnp.dot(residual, basis, precision=highest, preferred_element_type=jnp.float32)
            / feat_count
        )
        coef = lax.dot_general(proj, basis, (((1,), (1,)), ((), ())), precision=highest)
        solved = ridge_solve(factor, coef)
        back = jnp.dot(solved, basis, precision=highest, preferred_element_type=jnp.float32)
        local = weights + (proj - back) / ridge
        summed, primal_groups = lax.psum((local, primal_part), "frames")
        updated = penalty / (ridge_weight + penalty * group_count) * summed
        moved = updated - weights
        change, primal = lax.psum((jnp.sum(moved * moved), primal_groups), "feat")
        ratio = (primal / (total_frames * class_count) + epsilon) / (
            group_count * penalty * penalty * change / (total_features * class_count) + epsilon
        )
        next_penalty = penalty * jnp.sqrt(jnp.sqrt(ratio))
        duals = duals * (penalty / next_penalty)
        penalty = next_penalty
        weights = updated
    duals = lax.dynamic_slice_in_dim(duals, offset, share, 1)
    return (weights, duals, penalty)


def solution(mesh):
    return jax.shard_map(
        shards,
        mesh=mesh,
        in_specs=(
            P("frames", None),
            P(None, "feat"),
            P("feat"),
            P("frames"),
            P(None, "feat"),
            P(None, "frames"),
        ),
        out_specs=(P(None, "feat"), P(None, ("frames", "feat")), P()),
        check_vma=False,
    )
```

profile of v0, /device:TPU:0, one launch (start us, length us, event | category | flops | bytes accessed | tf_op | source)
XLA Modules:
  0.0 297.5 jit_solution(15187236382029461404)
XLA Ops:
  7.2 0.0 all-reduce.8.cloned.1.call-start
  7.2 1.4 copy-done
  8.7 13.2 %fusion.1 = f32[256,1024]{1,0:T(8,128)S(1)} fusion(f32[256,440]{0,1:T(8,128)} %param.10, f32[440,1024]{1,0:T(8,128)S(1)} %copy-done, f32[1024]{0:T(1024)} %param.12), kind=kOutput, calls=%fused_computation.4 | convolution fusion | flops 1384644608 | bytes 3305472 | tf_op jit(solution)/shard_map/dot_general | solution.py:14
  21.8 1.9 convolution_bitcast_fusion
  23.7 0.0 all-reduce.8.cloned.1.call-update
  23.7 0.2 all-reduce.10.cloned.1.call-start
  24.0 1.7 fusion.69
  25.7 1.8 copy.9
  27.5 1.1 fusion.10
  28.6 0.7 copy-done.8
  29.3 0.6 cholesky.115
  29.9 12.5 %cholesky.49 = f32[128,128]{1,0:T(8,128)S(1)} custom-call(f32[128,128]{1,0:T(8,128)} %cholesky.115), custom_call_target="Cholesky" | custom-call | tf_op jit(solution)/shard_map/jit(cholesky)/cholesky | solution.py:54
  42.5 0.6 select_reduce_fusion.1
  43.1 11.3 %custom-call.17 = f32[1,128,128]{1,2,0:T(8,128)} custom-call(f32[1,128,128]{2,1,0:T(8,128)} %get-tuple-element.63), custom_call_target="InvertDiagBlocksLowerTriangular" | custom-call | tf_op jit(solution)/shard_map/jit(cholesky)/cholesky | solution.py:54
  54.4 0.7 cholesky.111
  55.1 1.7 constant_dynamic-update-slice_fusion
  56.8 1.7 convolution_subtract_fusion.6
  58.5 12.5 %cholesky.103 = f32[128,128]{1,0:T(8,128)S(1)} custom-call(f32[128,128]{1,0:T(8,128)} %convolution_subtract_fusion.6), custom_call_target="Cholesky" | custom-call | tf_op jit(solution)/shard_map/jit(cholesky)/cholesky | solution.py:54
  71.1 0.6 select_reduce_fusion
  71.7 0.7 compare_reduce_fusion
  73.8 1.7 select_select_fusion
  75.5 0.1 broadcast.169
  75.5 7.0 %while.8 = (s32[]{:T(128)}, f32[256,256]{1,0:T(8,128)}, s32[2,2]{1,0:T(2,128)S(1)}, f32[2,128,128]{2,1,0:T(8,128)}, s32[]{:T(128)}) while((s32[]{:T(128)}, f32[256,256]{1,0:T(8,128)}, s32[2,2]{1,0:T(2,128)S(1)}, f32[2,128,128]{2,1,0:T(8,128)}, s32[]{:T(128)}) %tuple.44), condition=%wide.while_cond, body=%wide.while_body.sunk | while | flops 2 | bytes 132205 | solution.py:21
  75.5 0.6 fusion.100
  76.1 2.9 bitcast_dynamic-update-slice_fusion.2
  79.1 0.6 fusion.100
  79.6 2.9 bitcast_dynamic-update-slice_fusion.2
  82.5 21.1 %custom-call.20 = f32[2,128,128]{1,2,0:T(8,128)} custom-call(f32[2,128,128]{2,1,0:T(8,128)} %get-tuple-element.33), custom_call_target="InvertDiagBlocksLowerTriangular" | custom-call | tf_op jit(solution)/shard_map/triangular_solve/custom-call.0 | solution.py:21
  103.6 1.7 fusion.66
  105.3 1.9 convolution_multiply_fusion.1
  107.2 1.2 fusion.70
  108.5 0.3 fusion.33
  108.8 0.3 convolution_subtract_fusion.5
  109.1 0.3 fusion.47
  109.3 0.3 fusion.48
  109.6 0.3 convolution_subtract_fusion.4
  109.9 0.3 fusion.44
  110.2 1.6 fusion.3
  111.9 0.0 all-reduce.12.cloned.1.call-start
  111.9 1.6 multiply_reduce_fusion.3
  113.5 9.0 %psum.71 = f32[]{:T(128)} all-reduce(f32[]{:T(128)} %multiply_reduce_fusion.3), channel_id=1, replica_groups=mesh['frames'=4,'feat'=8] {'frames'}, use_global_device_ids=true, to_apply=%region_2.3 | all-reduce | flops 1 | bytes 8 | tf_op jit(solution)/shard_map/psum | solution.py:73
  122.5 26.2 %all-reduce.10.cloned.1.call-done = f32[147,1024]{1,0:T(8,128)} async-done(((f32[147,1024]{1,0:T(8,128)}), f32[147,1024]{1,0:T(8,128)}) %all-reduce.10.cloned.1.call-update) | async-done | bytes 602128 | tf_op jit(solution)/shard_map/psum | solution.py:73
  148.7 3.0 %fusion.6 = f32[147,256]{1,0:T(8,128)} fusion(f32[256,1024]{1,0:T(8,128)S(1)} %fusion.1, f32[147,1024]{1,0:T(8,128)} %all-reduce.10.cloned.1.call-done), kind=kOutput, calls=%fused_computation.21 | convolution fusion | flops 462572544 | bytes 1801216 | tf_op jit(solution)/shard_map/dot_general | solution.py:60
  151.7 0.0 all-reduce.14.cloned.1.call-start
  151.8 1.8 multiply_reduce_fusion.1
  153.6 22.0 %all-reduce.2 = (f32[]{:T(128)}, f32[]{:T(128)}) all-reduce(f32[]{:T(128)} %psum.71, f32[]{:T(128)} %multiply_reduce_fusion.1), channel_id=1, replica_groups=mesh['frames'=4,'feat'=8] {'feat'}, use_global_device_ids=true, to_apply=%region_3.4 | all-reduce | flops 2 | bytes 16 | tf_op jit(solution)/shard_map/psum | solution.py:76
  177.1 45.5 %all-reduce.12.cloned.1.call-done = f32[147,256]{1,0:T(8,128)} async-done(((f32[147,256]{1,0:T(8,128)}), f32[147,256]{1,0:T(8,128)}) %all-reduce.12.cloned.1.call-update) | async-done | bytes 150544 | tf_op jit(solution)/shard_map/psum | solution.py:61
  222.6 1.9 convolution_multiply_fusion
  224.4 1.2 fusion.71
  225.7 0.3 fusion.31
  226.0 0.3 convolution_subtract_fusion.3
  226.3 0.3 fusion.45
  226.6 0.3 fusion.46
  226.9 0.3 convolution_subtract_fusion.2
  227.1 0.3 fusion.43
  227.4 1.6 fusion.5
  229.1 1.1 fusion.54
  230.2 0.7 multiply_reduce_fusion.2
  230.9 6.3 %psum.77 = f32[]{:T(128)} all-reduce(f32[]{:T(128)} %multiply_reduce_fusion.2), channel_id=1, replica_groups=mesh['frames'=4,'feat'=8] {'frames'}, use_global_device_ids=true, to_apply=%region_14.17 | all-reduce | flops 1 | bytes 8 | tf_op jit(solution)/shard_map/psum | solution.py:73
  237.2 25.8 %all-reduce.14.cloned.1.call-done = f32[147,1024]{1,0:T(8,128)} async-done(((f32[147,1024]{1,0:T(8,128)}), f32[147,1024]{1,0:T(8,128)}) %all-reduce.14.cloned.1.call-update) | async-done | bytes 602128 | tf_op jit(solution)/shard_map/psum | solution.py:73
  263.0 2.6 multiply_reduce_fusion
  265.6 22.0 %all-reduce.1 = (f32[]{:T(128)}, f32[]{:T(128)}) all-reduce(f32[]{:T(128)} %psum.77, f32[]{:T(128)} %get-tuple-element.52), channel_id=1, replica_groups=mesh['frames'=4,'feat'=8] {'feat'}, use_global_device_ids=true, to_apply=%region_15.18 | all-reduce | flops 2 | bytes 16 | tf_op jit(solution)/shard_map/psum | solution.py:76
  289.1 0.1 dynamic-slice_multiply_fusion
  289.2 0.7 copy.10
  (26 shorter events, 0.1 us)
Async XLA Ops:
  7.2 1.5 copy-start
  7.2 14.7 %copy-start.2 = (f32[147,1024]{1,0:T(8,128)S(1)}, f32[147,1024]{1,0:T(8,128)}, u32[]{:S(2)}) copy-start(f32[147,1024]{1,0:T(8,128)} %param.14) | copy-start | bytes 1806340
  7.2 96.4 %all-reduce.8.cloned.1.call-start = ((), (), s32[]{:S(2)}) async-start(), calls=%async_computation | async-start | bytes 311296 | tf_op jit(solution)/shard_map/psum | solution.py:61
  23.7 124.9 %all-reduce.10.cloned.1.call-start = ((), (), s32[]{:S(2)}) async-start(), calls=%async_computation.1 | async-start | bytes 1245184 | tf_op jit(solution)/shard_map/psum | solution.py:73
  27.5 76.1 %copy-start.9 = (s32[256]{0:T(256)S(1)}, s32[256]{0:T(256)}, u32[]{:S(2)}) copy-start(s32[256]{0:T(256)} %param.13) | copy-start | bytes 3076
  28.6 0.7 copy-start.8
  105.3 3.1 %copy-start.5 = (f32[147,256]{1,0:T(8,128)}, f32[147,256]{1,0:T(8,128)S(1)}, u32[]{:S(2)}) copy-start(f32[147,256]{1,0:T(8,128)S(1)} %get-tuple-element.54) | copy-start | bytes 451588
  105.3 3.1 %copy-start.6 = (f32[2,128,128]{1,2,0:T(8,128)S(1)}, f32[2,128,128]{1,2,0:T(8,128)}, u32[]{:S(2)}) copy-start(f32[2,128,128]{1,2,0:T(8,128)} %custom-call.20) | copy-start | bytes 393220
  105.3 3.4 %copy-start.3 = (f32[256,256]{1,0:T(8,128)S(1)}, f32[256,256]{1,0:T(8,128)}, u32[]{:S(2)}) copy-start(f32[256,256]{1,0:T(8,128)} %get-tuple-element.117) | copy-start | bytes 786436
  111.9 110.7 %all-reduce.12.cloned.1.call-start = ((), (), s32[]{:S(2)}) async-start(), calls=%async_computation.2 | async-start | bytes 311296 | tf_op jit(solution)/shard_map/psum | solution.py:61
  148.7 3.1 %copy-start.1 = (f32[147,1024]{1,0:T(8,128)S(1)}, f32[147,1024]{1,0:T(8,128)}, u32[]{:S(2)}) copy-start(f32[147,1024]{1,0:T(8,128)} %all-reduce.10.cloned.1.call-done) | copy-start | bytes 1806340
  151.7 111.3 %all-reduce.14.cloned.1.call-start = ((), (), s32[]{:S(2)}) async-start(), calls=%async_computation.3 | async-start | bytes 1245184 | tf_op jit(solution)/shard_map/psum | solution.py:73
  222.6 3.1 %copy-start.7 = (f32[2,128,128]{1,2,0:T(8,128)S(1)}, f32[2,128,128]{1,2,0:T(8,128)}, u32[]{:S(2)}) copy-start(f32[2,128,128]{1,2,0:T(8,128)} %custom-call.20) | copy-start | bytes 393220
  222.6 3.4 %copy-start.4 = (f32[256,256]{1,0:T(8,128)S(1)}, f32[256,256]{1,0:T(8,128)}, u32[]{:S(2)}) copy-start(f32[256,256]{1,0:T(8,128)} %get-tuple-element.117) | copy-start | bytes 786436
Sparse Core Ops, SparseCore 0:
  23.9 73.2 all-reduce.7
  112.0 36.6 all-reduce.9
  152.6 69.9 all-reduce.11
  229.2 33.7 all-reduce.13
where the time goes:
time: 299 us; the launch traced here: 298 us
  waiting for transfers between devices  97.5 us (33%)
  other arithmetic  71.9 us (24%)
  blocking collectives  59.2 us (20%)
  matrix products  36.1 us (12%)
  between operations  19.5 us (7%)
  local copies, waits for them, and re-layouts  13 us (4%)
    psum x2, waiting for transfers between devices, shards(): summed, primal_groups = lax.psum((local, primal_part), 'frames')  51.9 us
    psum x2, waiting for transfers between devices, shards(): predicted = lax.psum(partial_value, 'feat')  45.5 us
    psum x2, blocking collectives, shards(): change, primal = lax.psum((jnp.sum(moved * moved), primal_groups), 'feat')  44 us
    another operation x6, other arithmetic, shards(): factor = jnp.linalg.cholesky(inner_matrix)  38.4 us
    another operation x4, other arithmetic, ridge_solve(): lax.linalg.triangular_solve(factor, right, left_side=False, lower=True, t...  22.8 us
    psum x2, blocking collectives, shards(): summed, primal_groups = lax.psum((local, primal_part), 'frames')  15.3 us
    dot_general x1, matrix products, cosine_features(): jnp.dot(acoustic, projection, precision=highest, preferred_element_type=j...  13.2 us
    another operation x7, local copies, waits for them, and re-layouts, ridge_solve(): lax.linalg.triangular_solve(factor, right, left_side=False, lower=True, t...  7.03 us
  transfers between devices with their start and end apart: 4, of which 3 were waited for; matrix products, arithmetic and copies ran while one was open for 28% of the time, Pallas kernels for 0%

commit v1 on v0

--- a/solution.py
+++ b/solution.py
@@ -2,6 +2,7 @@
 import jax.numpy as jnp
 from jax import lax
 from jax.sharding import PartitionSpec as P
+from jax.lax import ppermute, psum
 
 ITERS = 2
 highest = lax.Precision.HIGHEST
@@ -58,7 +59,14 @@
     penalty = jnp.ones((), jnp.float32)
     for iteration in range(ITERS):
         partial_value = lax.dot_general(weights, basis, (((1,), (1,)), ((), ())), precision=highest)
-        predicted = lax.psum(partial_value, "feat")
+        n_axis = psum(1, axis_name="feat")
+        predicted, row_out = (partial_value, 0)
+        while 1 << row_out < n_axis:
+            x_next = ppermute(
+                predicted, axis_name="feat", perm=[(it, it ^ 1 << row_out) for it in range(n_axis)]
+            )
+            predicted = predicted + x_next
+            row_out = row_out + 1
         miss, duals, residual = proximal(predicted, duals, target, penalty)
         mine = lax.dynamic_slice_in_dim(miss, offset, share, 1)
         primal_part = jnp.sum(mine * mine)

time: 299 us -> 276 us (0.923)
  waiting for transfers between devices: 97.5 us -> 60.2 us
  starting transfers between devices: 0.34 us -> 12.7 us
  other arithmetic: 71.9 us -> 80.3 us
  blocking collectives: 59.2 us -> 53.9 us
    psum x2 -> x0, waiting for transfers between devices: 45.5 us -> none  [shards(): predicted = lax.psum(partial_value, 'feat')]
    ppermute x0 -> x6, starting transfers between devices: none -> 12.6 us  [shards(): ppermute(predicted, axis_name='feat', perm=[(it, it ^ 1 << row_out) for i...]
    ppermute x0 -> x6, waiting for transfers between devices: none -> 6.32 us  [shards(): ppermute(predicted, axis_name='feat', perm=[(it, it ^ 1 << row_out) for i...]
    add x0 -> x4, other arithmetic: none -> 5.69 us  [shards(): predicted = predicted + x_next]
  transfers between devices with their start and end apart: 4 -> 8, of which waited for: 3 -> 4; matrix products, arithmetic and copies ran while one was open for 28% -> 30% of each run, Pallas kernels for 0% -> 0%
where the time goes in v1:
time: 276 us; the launch traced here: 275 us
  other arithmetic  80.3 us (29%)
  waiting for transfers between devices  60.2 us (22%)
  blocking collectives  53.9 us (20%)
  matrix products  35.5 us (13%)
  between operations  19.7 us (7%)
  local copies, waits for them, and re-layouts  12.8 us (5%)
  starting transfers between devices  12.7 us (5%)
    psum x2, waiting for transfers between devices, shards(): summed, primal_groups = lax.psum((local, primal_part), 'frames')  53.8 us
    psum x2, blocking collectives, shards(): change, primal = lax.psum((jnp.sum(moved * moved), primal_groups), 'feat')  41.3 us
    another operation x6, other arithmetic, shards(): factor = jnp.linalg.cholesky(inner_matrix)  38.4 us
    another operation x4, other arithmetic, ridge_solve(): lax.linalg.triangular_solve(factor, right, left_side=False, lower=True, t...  22.8 us
    dot_general x1, matrix products, cosine_features(): jnp.dot(acoustic, projection, precision=highest, preferred_element_type=j...  13.3 us
    ppermute x6, starting transfers between devices, shards(): ppermute(predicted, axis_name='feat', perm=[(it, it ^ 1 << row_out) for i...  12.6 us
    psum x2, blocking collectives, shards(): summed, primal_groups = lax.psum((local, primal_part), 'frames')  12.6 us
    another operation x7, local copies, waits for them, and re-layouts, ridge_solve(): lax.linalg.triangular_solve(factor, right, left_side=False, lower=True, t...  6.82 us
  transfers between devices with their start and end apart: 8, of which 4 were waited for; matrix products, arithmetic and copies ran while one was open for 30% of the time, Pallas kernels for 0%

profile of v1, /device:TPU:0, one launch (start us, length us, event | category | flops | bytes accessed | tf_op | source)
XLA Modules:
  0.0 275.1 jit_solution(356546913883032916)
XLA Ops:
  7.2 1.4 copy-done
  8.7 13.3 %fusion.1 = f32[256,1024]{1,0:T(8,128)S(1)} fusion(f32[256,440]{0,1:T(8,128)} %param.10, f32[440,1024]{1,0:T(8,128)S(1)} %copy-done, f32[1024]{0:T(1024)} %param.12), kind=kOutput, calls=%fused_computation.4 | convolution fusion | flops 1384644608 | bytes 3305472 | tf_op jit(solution)/shard_map/dot_general | solution.py:15
  22.0 1.9 convolution_bitcast_fusion
  23.9 3.0 %collective-permute-start = (f32[147,256]{1,0:T(8,128)}, f32[147,256]{1,0:T(8,128)}, u32[]{:S(2)}, u32[]{:S(2)}) collective-permute-start(f32[147,256]{1,0:T(8,128)} %convolution_bitcast_fusion), channel_id=1, source_target_pairs={{0,1},{1,0},{2,3},{3,2},{4,5},{5,4},{6,7},{7,6},{8,9},{9,8},{10,11... | collective-permute-start | bytes 451592 | tf_op jit(solution)/shard_map/ppermute | solution.py:65
  26.9 1.7 fusion.69
  28.6 1.8 copy.9
  30.4 1.1 fusion.10
  31.5 0.7 copy-done.9
  32.2 0.6 cholesky.115
  32.8 12.5 %cholesky.49 = f32[128,128]{1,0:T(8,128)S(1)} custom-call(f32[128,128]{1,0:T(8,128)} %cholesky.115), custom_call_target="Cholesky" | custom-call | tf_op jit(solution)/shard_map/jit(cholesky)/cholesky | solution.py:55
  45.4 0.6 select_reduce_fusion.1
  46.0 11.3 %custom-call.17 = f32[1,128,128]{1,2,0:T(8,128)} custom-call(f32[1,128,128]{2,1,0:T(8,128)} %get-tuple-element.64), custom_call_target="InvertDiagBlocksLowerTriangular" | custom-call | tf_op jit(solution)/shard_map/jit(cholesky)/cholesky | solution.py:55
  57.3 0.7 cholesky.111
  58.0 1.7 constant_dynamic-update-slice_fusion
  59.7 1.7 convolution_subtract_fusion.6
  61.4 12.7 %cholesky.103 = f32[128,128]{1,0:T(8,128)S(1)} custom-call(f32[128,128]{1,0:T(8,128)} %convolution_subtract_fusion.6), custom_call_target="Cholesky" | custom-call | tf_op jit(solution)/shard_map/jit(cholesky)/cholesky | solution.py:55
  74.1 0.6 select_reduce_fusion
  74.8 0.6 compare_reduce_fusion
  76.7 1.7 add.119
  78.4 1.6 collective-permute-start.1
  79.9 1.7 select_select_fusion
  81.6 2.6 collective-permute-done.1
  84.2 1.7 add.120
  85.8 2.6 collective-permute-start.2
  88.5 6.8 %while.8 = (s32[]{:T(128)}, f32[256,256]{1,0:T(8,128)}, s32[2,2]{1,0:T(2,128)S(1)}, f32[2,128,128]{2,1,0:T(8,128)}, s32[]{:T(128)}) while((s32[]{:T(128)}, f32[256,256]{1,0:T(8,128)}, s32[2,2]{1,0:T(2,128)S(1)}, f32[2,128,128]{2,1,0:T(8,128)}, s32[]{:T(128)}) %tuple.45), condition=%wide.while_cond, body=%wide.while_body.sunk | while | flops 2 | bytes 132205 | solution.py:22
  88.5 0.6 fusion.100
  89.1 2.8 %bitcast_dynamic-update-slice_fusion.2 = f32[2,128,128]{2,1,0:T(8,128)} fusion(f32[2,128,128]{2,1,0:T(8,128)} %get-tuple-element.106, s32[]{:T(128)S(6)} %copy.16, f32[256,256]{1,0:T(8,128)} %get-tuple-element.109, s32[]{:T(128)} %bitcast.83, s32[]{:T(128)} %bitcast.84), kind=kLoop, calls=%fused_computation.clone.1 | loop fusion | bytes 132100 | tf_op jit(solution)/shard_map/triangular_solve | solution.py:22
  91.9 0.6 fusion.100
  92.5 2.8 %bitcast_dynamic-update-slice_fusion.2 = f32[2,128,128]{2,1,0:T(8,128)} fusion(f32[2,128,128]{2,1,0:T(8,128)} %get-tuple-element.106, s32[]{:T(128)S(6)} %copy.16, f32[256,256]{1,0:T(8,128)} %get-tuple-element.109, s32[]{:T(128)} %bitcast.83, s32[]{:T(128)} %bitcast.84), kind=kLoop, calls=%fused_computation.clone.1 | loop fusion | bytes 132100 | tf_op jit(solution)/shard_map/triangular_solve | solution.py:22
  95.3 21.1 %custom-call.20 = f32[2,128,128]{1,2,0:T(8,128)} custom-call(f32[2,128,128]{2,1,0:T(8,128)} %get-tuple-element.33), custom_call_target="InvertDiagBlocksLowerTriangular" | custom-call | tf_op jit(solution)/shard_map/triangular_solve/custom-call.0 | solution.py:22
  116.4 1.8 fusion.66
  118.2 1.8 convolution_multiply_fusion.1
  120.0 1.2 fusion.70
  121.5 0.3 convolution_subtract_fusion.5
  122.1 0.3 fusion.48
  122.4 0.3 convolution_subtract_fusion.4
  122.7 0.3 fusion.44
  123.0 1.6 fusion.3
  124.7 32.3 %all-reduce.6.cloned.1.call-done = f32[147,1024]{1,0:T(8,128)} async-done(((f32[147,1024]{1,0:T(8,128)}), f32[147,1024]{1,0:T(8,128)}) %all-reduce.6.cloned.1.call-update) | async-done | bytes 602128 | tf_op jit(solution)/shard_map/psum | solution.py:81
  157.0 2.4 fusion.6
  159.3 1.5 collective-permute-start.3
  160.9 3.8 %collective-permute-done.3 = f32[147,256]{1,0:T(8,128)S(1)} collective-permute-done((f32[147,256]{1,0:T(8,128)S(1)}, f32[147,256]{1,0:T(8,128)S(1)}, u32[]{:S(2)}, u32[]{:S(2)}) %collective-permute-start.3) | collective-permute-done | bytes 150560 | tf_op jit(solution)/shard_map/ppermute | solution.py:65
  164.6 0.7 add.133
  165.3 1.5 collective-permute-start.4
  166.8 1.6 multiply_reduce_fusion.3
  168.4 6.3 %psum.56 = f32[]{:T(128)} all-reduce(f32[]{:T(128)} %multiply_reduce_fusion.3), channel_id=1, replica_groups=mesh['frames'=4,'feat'=8] {'frames'}, use_global_device_ids=true, to_apply=%region_1.2 | all-reduce | flops 1 | bytes 8 | tf_op jit(solution)/shard_map/psum | solution.py:81
  174.6 1.7 add.134
  176.3 2.4 collective-permute-start.5
  178.7 1.8 multiply_reduce_fusion.1
  180.6 19.3 %all-reduce.2 = (f32[]{:T(128)}, f32[]{:T(128)}) all-reduce(f32[]{:T(128)} %psum.56, f32[]{:T(128)} %multiply_reduce_fusion.1), channel_id=1, replica_groups=mesh['frames'=4,'feat'=8] {'feat'}, use_global_device_ids=true, to_apply=%region_2.3 | all-reduce | flops 2 | bytes 16 | tf_op jit(solution)/shard_map/psum | solution.py:84
  201.4 1.8 fusion.54
  203.2 1.8 convolution_multiply_fusion
  205.0 1.2 fusion.71
  206.5 0.3 convolution_subtract_fusion.3
  207.1 0.3 fusion.46
  207.7 0.3 fusion.43
  208.0 1.6 fusion.5
  209.7 1.6 multiply_reduce_fusion.2
  211.3 6.3 %psum.61 = f32[]{:T(128)} all-reduce(f32[]{:T(128)} %multiply_reduce_fusion.2), channel_id=1, replica_groups=mesh['frames'=4,'feat'=8] {'frames'}, use_global_device_ids=true, to_apply=%region_12.15 | all-reduce | flops 1 | bytes 8 | tf_op jit(solution)/shard_map/psum | solution.py:81
  217.6 1.1 multiply_add_fusion
  218.7 21.5 %all-reduce.8.cloned.1.call-done = f32[147,1024]{1,0:T(8,128)} async-done(((f32[147,1024]{1,0:T(8,128)}), f32[147,1024]{1,0:T(8,128)}) %all-reduce.8.cloned.1.call-update) | async-done | bytes 602128 | tf_op jit(solution)/shard_map/psum | solution.py:81
  240.3 2.6 multiply_reduce_fusion
  242.9 22.0 %all-reduce.1 = (f32[]{:T(128)}, f32[]{:T(128)}) all-reduce(f32[]{:T(128)} %psum.61, f32[]{:T(128)} %get-tuple-element.52), channel_id=1, replica_groups=mesh['frames'=4,'feat'=8] {'feat'}, use_global_device_ids=true, to_apply=%region_13.16 | all-reduce | flops 2 | bytes 16 | tf_op jit(solution)/shard_map/psum | solution.py:84
  266.4 0.7 copy.10
  (39 shorter events, 1.7 us)
Async XLA Ops:
  7.2 1.5 copy-start
  7.2 14.8 %copy-start.2 = (f32[147,1024]{1,0:T(8,128)S(1)}, f32[147,1024]{1,0:T(8,128)}, u32[]{:S(2)}) copy-start(f32[147,1024]{1,0:T(8,128)} %param.14) | copy-start | bytes 1806340
  7.2 149.8 %all-reduce.6.cloned.1.call-start = ((), (), s32[]{:S(2)}) async-start(), calls=%async_computation | async-start | bytes 1245184 | tf_op jit(solution)/shard_map/psum | solution.py:81
  23.9 52.8 %collective-permute-start = (f32[147,256]{1,0:T(8,128)}, f32[147,256]{1,0:T(8,128)}, u32[]{:S(2)}, u32[]{:S(2)}) collective-permute-start(f32[147,256]{1,0:T(8,128)} %convolution_bitcast_fusion), channel_id=1, source_target_pairs={{0,1},{1,0},{2,3},{3,2},{4,5},{5,4},{6,7},{7,6},{8,9},{9,8},{10,11... | collective-permute-start | bytes 451592 | tf_op jit(solution)/shard_map/ppermute | solution.py:65
  31.5 0.7 copy-start.9
  32.2 84.2 %copy-start.10 = (s32[256]{0:T(256)S(1)}, s32[256]{0:T(256)}, u32[]{:S(2)}) copy-start(s32[256]{0:T(256)} %param.13) | copy-start | bytes 3076
  78.4 5.8 %collective-permute-start.1 = (f32[147,256]{1,0:T(8,128)}, f32[147,256]{1,0:T(8,128)}, u32[]{:S(2)}, u32[]{:S(2)}) collective-permute-start(f32[147,256]{1,0:T(8,128)} %add.119), channel_id=1, source_target_pairs={{0,2},{1,3},{2,0},{3,1},{4,6},{5,7},{6,4},{7,5},{8,10},{9,11},{10,... | collective-permute-start | bytes 451592 | tf_op jit(solution)/shard_map/ppermute | solution.py:65
  85.8 30.5 %collective-permute-start.2 = (f32[147,256]{1,0:T(8,128)}, f32[147,256]{1,0:T(8,128)}, u32[]{:S(2)}, u32[]{:S(2)}) collective-permute-start(f32[147,256]{1,0:T(8,128)} %add.120), channel_id=1, source_target_pairs={{0,4},{1,5},{2,6},{3,7},{4,0},{5,1},{6,2},{7,3},{8,12},{9,13},{10,... | collective-permute-start | bytes 451592 | tf_op jit(solution)/shard_map/ppermute | solution.py:65
  118.1 3.0 %copy-start.3 = (f32[147,256]{1,0:T(8,128)}, f32[147,256]{1,0:T(8,128)S(1)}, u32[]{:S(2)}) copy-start(f32[147,256]{1,0:T(8,128)S(1)} %get-tuple-element.56) | copy-start | bytes 451588
  118.2 3.0 %copy-start.6 = (f32[2,128,128]{1,2,0:T(8,128)S(1)}, f32[2,128,128]{1,2,0:T(8,128)}, u32[]{:S(2)}) copy-start(f32[2,128,128]{1,2,0:T(8,128)} %custom-call.20) | copy-start | bytes 393220
  118.2 3.3 %copy-start.4 = (f32[256,256]{1,0:T(8,128)S(1)}, f32[256,256]{1,0:T(8,128)}, u32[]{:S(2)}) copy-start(f32[256,256]{1,0:T(8,128)} %get-tuple-element.116) | copy-start | bytes 786436
  124.6 115.6 %all-reduce.8.cloned.1.call-start = ((), (), s32[]{:S(2)}) async-start(), calls=%async_computation.1 | async-start | bytes 1245184 | tf_op jit(solution)/shard_map/psum | solution.py:81
  157.0 21.8 %copy-start.1 = (f32[147,1024]{1,0:T(8,128)S(1)}, f32[147,1024]{1,0:T(8,128)}, u32[]{:S(2)}) copy-start(f32[147,1024]{1,0:T(8,128)} %all-reduce.6.cloned.1.call-done) | copy-start | bytes 1806340
  159.3 5.3 %collective-permute-start.3 = (f32[147,256]{1,0:T(8,128)S(1)}, f32[147,256]{1,0:T(8,128)S(1)}, u32[]{:S(2)}, u32[]{:S(2)}) collective-permute-start(f32[147,256]{1,0:T(8,128)S(1)} %fusion.6), channel_id=1, source_target_pairs={{0,1},{1,0},{2,3},{3,2},{4,5},{5,4},{6,7},{7,6},{8,9},{9,8},{10,11... | collective-permute-start | bytes 451592 | tf_op jit(solution)/shard_map/ppermute | solution.py:65
  165.3 9.3 %collective-permute-start.4 = (f32[147,256]{1,0:T(8,128)}, f32[147,256]{1,0:T(8,128)}, u32[]{:S(2)}, u32[]{:S(2)}) collective-permute-start(f32[147,256]{1,0:T(8,128)} %add.133), channel_id=1, source_target_pairs={{0,2},{1,3},{2,0},{3,1},{4,6},{5,7},{6,4},{7,5},{8,10},{9,11},{10,... | collective-permute-start | bytes 451592 | tf_op jit(solution)/shard_map/ppermute | solution.py:65
  176.3 25.0 %collective-permute-start.5 = (f32[147,256]{1,0:T(8,128)}, f32[147,256]{1,0:T(8,128)}, u32[]{:S(2)}, u32[]{:S(2)}) collective-permute-start(f32[147,256]{1,0:T(8,128)} %add.134), channel_id=1, source_target_pairs={{0,4},{1,5},{2,6},{3,7},{4,0},{5,1},{6,2},{7,3},{8,12},{9,13},{10,... | collective-permute-start | bytes 451592 | tf_op jit(solution)/shard_map/ppermute | solution.py:65
  203.2 3.1 %copy-start.8 = (f32[147,256]{1,0:T(8,128)}, f32[147,256]{1,0:T(8,128)S(1)}, u32[]{:S(2)}) copy-start(f32[147,256]{1,0:T(8,128)S(1)} %get-tuple-element.55) | copy-start | bytes 451588
  203.2 3.1 %copy-start.7 = (f32[2,128,128]{1,2,0:T(8,128)S(1)}, f32[2,128,128]{1,2,0:T(8,128)}, u32[]{:S(2)}) copy-start(f32[2,128,128]{1,2,0:T(8,128)} %custom-call.20) | copy-start | bytes 393220
  203.2 3.4 %copy-start.5 = (f32[256,256]{1,0:T(8,128)S(1)}, f32[256,256]{1,0:T(8,128)}, u32[]{:S(2)}) copy-start(f32[256,256]{1,0:T(8,128)} %get-tuple-element.116) | copy-start | bytes 786436
Sparse Core Ops, SparseCore 0:
  124.7 32.1 all-reduce.5
  209.8 30.3 all-reduce.7
